TPU v7x, 32 devices: a whole 2x2x4 slice. The times are simulated.
32 devices in a mesh: grp: 2 (over x), yz: 8 (over z, y), gx: 2 (over core).
Axes of the slice: x: 2, y: 2, z: 4, core: 2. Of those that a mesh axis runs over, the one named last changes fastest.
Arguments:
- field: bfloat16 [4096, 256, 128], P(('grp', 'gx'), 'yz'), parts along dimension 0, may hold values from -6 to 6
- sketch_seeds: int32 [12], P('grp'), parts along dimension 0, may hold values from 1 to 32748
Outputs:
- basis: float32 [4096, 256], P(('grp', 'gx')), parts along dimension 0
- core: bfloat16 [512, 256, 128], P(('grp', 'gx'), 'yz'), parts along dimension 0
There are 2 independent parts, one for each index of `grp`. A program takes and returns all parts, laid end to end along the dimension named above; each array names one. Nothing has to cross between parts.
All inputs are finite; a program needn't handle non-finite values.
Results may differ from a plain program's by a relative error of at most 0.0057.
Values sent between devices are 32-bit elements; how exact they have to be, the bound alone decides.
No kernel may reach another device: no remote copies, remote signals or barrier semaphores. Data moves between devices by JAX's collectives and lax.ppermute only.
A program may use at most 64 MiB of HBM per device.

v0:
```python
import math
import jax
import jax.numpy as jnp
from jax import lax
from jax.sharding import PartitionSpec as P

RANK = 256
prime = 32749


def omega_table(seeds, start, count):
    place = (start + jnp.arange(count, dtype=jnp.int32) + 1)[:, None]
    column = (jnp.arange(RANK, dtype=jnp.int32) + 1)[None, :]
    first = seeds[0] * place % prime
    second = (seeds[1] * column + seeds[2]) % prime
    square = place * place % prime
    third = seeds[2] * column % prime
    mixed = (first * second % prime + square * third % prime) % prime
    return mixed.astype(jnp.float32) * (2.0 / prime) - 1.0


def local(field, sketch_seeds):
    x_local, y_local, z_local = field.shape
    y_start = lax.axis_index("yz") * y_local
    omega_z = omega_table(sketch_seeds[3:6], 0, z_local).astype(jnp.bfloat16)
    omega_y = omega_table(sketch_seeds[0:3], y_start, y_local)
    block = math.gcd(y_local, 8)

    def add_block(total, index):
        rows = lax.dynamic_slice_in_dim(field, index * block, block, 1)
        proj = jnp.dot(
            rows.reshape(x_local * block, z_local), omega_z, preferred_element_type=jnp.float32
        ).reshape(x_local, block, RANK)
        weight_y = lax.dynamic_slice_in_dim(omega_y, index * block, block, 0)
        return (total + jnp.sum(proj * weight_y[None], axis=1), None)

    partial_value, unused = lax.scan(
        add_block,
        jnp.zeros((x_local, RANK), jnp.float32),
        jnp.arange(y_local // block, dtype=jnp.int32),
    )
    sketch = lax.psum(partial_value, "yz")
    gram = lax.psum(
        jnp.dot(
            sketch.T, sketch, precision=lax.Precision.HIGHEST, preferred_element_type=jnp.float32
        ),
        "gx",
    )
    lower = jnp.linalg.cholesky(gram)
    basis = lax.linalg.triangular_solve(
        lower, sketch, left_side=False, lower=True, transpose_a=True
    )
    basis_half = basis.astype(jnp.bfloat16)
    flat = field.reshape(x_local, y_local * z_local)
    owned_rank = RANK // lax.axis_size("gx")
    core = lax.psum_scatter(
        lax.dot_general(
            basis_half, flat, (((0,), (0,)), ((), ())), preferred_element_type=jnp.float32
        ),
        "gx",
        scatter_dimension=0,
        tiled=True,
    )
    return (basis, core.reshape(owned_rank, y_local, z_local).astype(jnp.bfloat16))


def solution(mesh):
    in_specs = (P(("grp", "gx"), "yz", None), P("grp"))
    out_specs = (P(("grp", "gx"), None), P(("grp", "gx"), "yz", None))
    return jax.shard_map(local, mesh=mesh, in_specs=in_specs, out_specs=out_specs, check_vma=False)
```

profile of v0, /device:TPU:0, one launch (start us, length us, event | category | flops | bytes accessed | tf_op | source)
XLA Modules:
  0.0 233.7 jit_solution(5224184737601147460)
XLA Ops:
  7.2 1.6 fusion.53
  8.8 0.7 and_select_fusion.5
  9.5 0.6 and_select_fusion.1
  10.1 1.3 and_select_fusion.4
  11.4 1.2 and_select_fusion
  12.8 20.5 %while.13 = (s32[]{:T(128)}, f32[1024,256]{1,0:T(8,128)S(1)}, s32[4]{0:T(128)S(1)}, bf16[1024,32,128]{2,1,0:T(8,128)(2,1)}, f32[32,256]{1,0:T(8,128)S(1)}, /*ind...) while((s32[]{:T(128)}, f32[1024,256]{1,0:T(8,128)S(1)}, ...), condition=%wide.region_2.3_spmd.clone, body=%wide.region_0.2_spmd.clone.sunk | while | flops 542146560 | bytes 10513617 | solution.py:37
  12.8 0.7 dynamic_slice.20
  14.1 1.7 constant_dynamic-slice_fusion.8
  15.9 1.7 multiply_reduce_fusion.2
  17.6 0.3 select_add_fusion.2
  17.9 0.7 dynamic_slice.20
  19.3 1.7 constant_dynamic-slice_fusion.8
  21.0 1.7 multiply_reduce_fusion.2
  22.7 0.3 select_add_fusion.2
  23.0 0.7 dynamic_slice.20
  24.4 1.7 constant_dynamic-slice_fusion.8
  26.1 1.7 multiply_reduce_fusion.2
  27.9 0.3 select_add_fusion.2
  28.2 0.7 dynamic_slice.20
  29.5 1.7 constant_dynamic-slice_fusion.8
  31.3 1.7 multiply_reduce_fusion.2
  33.0 0.3 select_add_fusion.2
  33.3 1.0 copy-done
  34.3 81.1 %all-reduce.4.cloned.1.call-done = f32[1024,256]{1,0:T(8,128)} async-done(((f32[1024,256]{1,0:T(8,128)}), f32[1024,256]{1,0:T(8,128)}) %all-reduce.4.cloned.1.call-update) | async-done | bytes 1048592 | tf_op jit(solution)/shard_map/psum | solution.py:42
  115.4 4.1 %fusion.54 = f32[256,256]{0,1:T(8,128)} fusion(f32[1024,256]{1,0:T(8,128)} %all-reduce.4.cloned.1.call-done), kind=kOutput, calls=%fused_computation.98 | convolution fusion | flops 805306368 | bytes 1310720 | tf_op jit(solution)/shard_map/dot_general | solution.py:44
  119.8 17.7 %all-reduce.6.cloned.1.call-done = f32[256,256]{0,1:T(8,128)} async-done(((f32[256,256]{0,1:T(8,128)}), f32[256,256]{0,1:T(8,128)}) %all-reduce.6.cloned.1.call-update) | async-done | bytes 262160 | tf_op jit(solution)/shard_map/psum | solution.py:43
  137.6 1.1 copy.6
  138.6 1.0 fusion.35
  139.6 11.7 %cholesky.50 = f32[128,128]{1,0:T(8,128)S(1)} custom-call(f32[128,128]{1,0:T(8,128)S(1)} %cholesky.118), custom_call_target="Cholesky" | custom-call | tf_op jit(solution)/shard_map/jit(cholesky)/cholesky | solution.py:49
  151.4 0.6 compare_reduce_fusion.1
  152.0 9.8 %custom-call.14 = f32[1,128,128]{1,2,0:T(8,128)S(1)} custom-call(f32[1,128,128]{2,1,0:T(8,128)S(1)} %get-tuple-element.121), custom_call_target="InvertDiagBlocksLowerTriangular" | custom-call | tf_op jit(solution)/shard_map/jit(cholesky)/cholesky | solution.py:49
  162.1 0.3 convolution_subtract_fusion.1
  162.4 11.7 %cholesky.105 = f32[128,128]{1,0:T(8,128)S(1)} custom-call(f32[128,128]{1,0:T(8,128)S(1)} %convolution_subtract_fusion.1), custom_call_target="Cholesky" | custom-call | tf_op jit(solution)/shard_map/jit(cholesky)/cholesky | solution.py:49
  174.1 0.7 compare_reduce_fusion
  176.3 4.3 %while.12 = (s32[]{:T(128)}, f32[256,256]{1,0:T(8,128)S(1)}, s32[2,2]{1,0:T(2,128)S(1)}, f32[2,128,128]{2,1,0:T(8,128)S(1)}, s32[]{:T(128)}) while((s32[]{:T(128)}, f32[256,256]{1,0:T(8,128)S(1)}, s32[2,2]{1,0:T(2,128)S(1)}, f32[2,128,128]{2,1,0:T(8,128)S(1)}, s32[]{:T(128)}) %tuple.57), condition=%wide.while_cond, body=%wide.while_body.sunk | while | flops 2 | bytes 131189 | solution.py:50
  176.5 0.6 fusion.64
  177.1 1.4 bitcast_dynamic-update-slice_fusion.2
  178.5 0.6 fusion.64
  179.1 1.4 bitcast_dynamic-update-slice_fusion.2
  180.5 19.7 %custom-call.15 = f32[2,128,128]{1,2,0:T(8,128)S(1)} custom-call(f32[2,128,128]{2,1,0:T(8,128)S(1)} %get-tuple-element.42), custom_call_target="InvertDiagBlocksLowerTriangular" | custom-call | tf_op jit(solution)/shard_map/triangular_solve | solution.py:50
  200.2 0.6 fusion.32
  200.9 1.0 convolution_subtract_fusion
  201.9 0.6 fusion.36
  202.5 8.3 %fusion.29 = f32[256,4096]{1,0:T(8,128)} fusion(bf16[128,8,32,128]{3,2,1,0:T(8,128)(2,1)} %bitcast.54, f32[1024,128]{0,1:T(8,128)S(1)} %fusion.36, f32[1024,128]{0,1:T(8,128)S(1)} %fusion.32), kind=kOutput, calls=%fused_computation.38 | convolution fusion | flops 2148532224 | bytes 13631488 | tf_op jit(solution)/shard_map/dot_general | solution.py:57
  210.9 1.3 copy.7
  212.2 12.0 %reduce-scatter.2.cloned.1.call-done = f32[128,4096]{1,0:T(8,128)} async-done(((f32[256,4096]{1,0:T(8,128)}), f32[128,4096]{1,0:T(8,128)}) %reduce-scatter.2.cloned.1.call-update) | async-done | bytes 2097168 | tf_op jit(solution)/shard_map/reduce_scatter | solution.py:56
  224.2 1.8 convert_bitcast_fusion
  226.0 1.2 copy.11
  (28 shorter events, 1.1 us)
Async XLA Ops:
  7.2 108.2 %all-reduce.4.cloned.1.call-start = ((), (), s32[]{:S(2)}) async-start(), calls=%async_computation.1 | async-start | bytes 2097152 | tf_op jit(solution)/shard_map/psum | solution.py:42
  33.3 1.0 copy-start
  34.3 103.3 %all-reduce.6.cloned.1.call-start = ((), (), s32[]{:S(2)}) async-start(), calls=%async_computation.2 | async-start | bytes 524288 | tf_op jit(solution)/shard_map/psum | solution.py:43
  115.4 84.8 %copy-start.1 = (f32[1024,256]{1,0:T(8,128)S(1)}, f32[1024,256]{1,0:T(8,128)}, u32[]{:S(2)}) copy-start(f32[1024,256]{1,0:T(8,128)} %all-reduce.4.cloned.1.call-done) | copy-start | bytes 3145732
  119.6 104.6 %reduce-scatter.2.cloned.1.call-start = ((), (), s32[]{:S(2)}) async-start(), calls=%async_computation.3 | async-start | bytes 6291456 | tf_op jit(solution)/shard_map/reduce_scatter | solution.py:56
Sparse Core Ops, SparseCore 0:
  34.4 80.9 all-reduce.3
  119.7 17.8 all-reduce.5
  210.9 13.2 reduce-scatter.1
where the time goes:
time: 234 us
  waiting for transfers between devices  111 us (47%)
  other arithmetic  62.3 us (27%)
  matrix products  21.9 us (9%)
  local copies, waits for them, and re-layouts  19.9 us (9%)
  between operations  15.3 us (7%)
  loops' own time  3.19 us (1%)
    psum x1, waiting for transfers between devices, local(): sketch = lax.psum(partial_value, 'yz')  81.1 us
    another operation x7, other arithmetic, local(): lower = jnp.linalg.cholesky(gram)  34.7 us
    another operation x4, other arithmetic, local(): lax.linalg.triangular_solve(lower, sketch, left_side=False, lower=True, t...  19.8 us
    psum x1, waiting for transfers between devices, local(): lax.psum(jnp.dot(sketch.T, sketch, precision=lax.Precision.HIGHEST, prefe...  17.7 us
    reduce_scatter x1, waiting for transfers between devices, local(): lax.psum_scatter(lax.dot_general(basis_half, flat, (((0,), (0,)), ((), ()...  12 us
    dot_general x1, matrix products, local(): lax.dot_general(basis_half, flat, (((0,), (0,)), ((), ())), preferred_ele...  8.29 us
    dynamic_slice x4, local copies, waits for them, and re-layouts, add_block(): rows = lax.dynamic_slice_in_dim(field, index * block, block, 1)  6.93 us
    dot_general x4, matrix products, add_block(): jnp.dot(rows.reshape(x_local * block, z_local), omega_z, preferred_elemen...  6.81 us
  transfers between devices with their start and end apart: 3, of which 3 were waited for; matrix products, arithmetic and copies ran while one was open for 1% of the time, Pallas kernels for 0%

commit v1 on v0

--- a/solution.py
+++ b/solution.py
@@ -40,12 +40,11 @@
         jnp.arange(y_local // block, dtype=jnp.int32),
     )
     sketch = lax.psum(partial_value, "yz")
-    gram = lax.psum(
-        jnp.dot(
-            sketch.T, sketch, precision=lax.Precision.HIGHEST, preferred_element_type=jnp.float32
-        ),
-        "gx",
+    own = jnp.dot(
+        sketch.T, sketch, precision=lax.Precision.HIGHEST, preferred_element_type=jnp.float32
     )
+    blocks = lax.all_gather(own, "gx", axis=0, tiled=False)
+    gram = blocks.sum(axis=0)
     lower = jnp.linalg.cholesky(gram)
     basis = lax.linalg.triangular_solve(
         lower, sketch, left_side=False, lower=True, transpose_a=True

time: 234 us -> 215 us (0.919)
  waiting for transfers between devices: 111 us -> 91.5 us
  blocking collectives: 0 us -> 2.36 us
    psum x1 -> x0, waiting for transfers between devices: 17.7 us -> none  [local(): lax.psum(jnp.dot(sketch.T, sketch, precision=lax.Precision.HIGHEST, prefe...]
    all_gather x0 -> x1, blocking collectives: none -> 2.36 us  [local(): blocks = lax.all_gather(own, 'gx', axis=0, tiled=False)]
  transfers between devices with their start and end apart: 3 -> 2, of which waited for: 3 -> 2; matrix products, arithmetic and copies ran while one was open for 1% -> 1% of each run, Pallas kernels for 0% -> 0%
where the time goes in v1:
time: 215 us; the launch traced here: 214 us
  waiting for transfers between devices  91.5 us (43%)
  other arithmetic  61.3 us (29%)
  matrix products  21.3 us (10%)
  local copies, waits for them, and re-layouts  18.9 us (9%)
  between operations  15.6 us (7%)
  loops' own time  3.19 us (1%)
  blocking collectives  2.36 us (1%)
    psum x1, waiting for transfers between devices, local(): sketch = lax.psum(partial_value, 'yz')  81.1 us
    another operation x7, other arithmetic, local(): lower = jnp.linalg.cholesky(gram)  34.7 us
    another operation x4, other arithmetic, local(): lax.linalg.triangular_solve(lower, sketch, left_side=False, lower=True, t...  19.8 us
    reduce_scatter x1, waiting for transfers between devices, local(): lax.psum_scatter(lax.dot_general(basis_half, flat, (((0,), (0,)), ((), ()...  10.4 us
    dot_general x1, matrix products, local(): lax.dot_general(basis_half, flat, (((0,), (0,)), ((), ())), preferred_ele...  8.3 us
    dynamic_slice x4, local copies, waits for them, and re-layouts, add_block(): rows = lax.dynamic_slice_in_dim(field, index * block, block, 1)  6.93 us
    dot_general x4, matrix products, add_block(): jnp.dot(rows.reshape(x_local * block, z_local), omega_z, preferred_elemen...  6.81 us
  transfers between devices with their start and end apart: 2, of which 2 were waited for; matrix products, arithmetic and copies ran while one was open for 1% of the time, Pallas kernels for 0%

profile of v1, /device:TPU:0, one launch (start us, length us, event | category | flops | bytes accessed | tf_op | source)
XLA Modules:
  0.0 214.2 jit_solution(5610417340013014138)
XLA Ops:
  7.2 1.6 fusion.53
  8.8 0.7 and_select_fusion.5
  9.5 0.6 and_select_fusion.1
  10.1 1.3 and_select_fusion.4
  11.4 1.2 and_select_fusion
  12.6 0.1 fusion.45
  12.8 20.5 %while.13 = (s32[]{:T(128)}, f32[1024,256]{1,0:T(8,128)S(1)}, s32[4]{0:T(128)S(1)}, bf16[1024,32,128]{2,1,0:T(8,128)(2,1)}, f32[32,256]{1,0:T(8,128)S(1)}, /*ind...) while((s32[]{:T(128)}, f32[1024,256]{1,0:T(8,128)S(1)}, ...), condition=%wide.region_2.3_spmd.clone, body=%wide.region_0.2_spmd.clone.sunk | while | flops 542146560 | bytes 10513617 | solution.py:37
  12.8 0.7 dynamic_slice.20
  14.1 1.7 constant_dynamic-slice_fusion.8
  15.9 1.7 multiply_reduce_fusion.2
  17.6 0.3 select_add_fusion.2
  17.9 0.7 dynamic_slice.20
  19.3 1.7 constant_dynamic-slice_fusion.8
  21.0 1.7 multiply_reduce_fusion.2
  22.7 0.3 select_add_fusion.2
  23.0 0.7 dynamic_slice.20
  24.4 1.7 constant_dynamic-slice_fusion.8
  26.1 1.7 multiply_reduce_fusion.2
  27.9 0.3 select_add_fusion.2
  28.2 0.7 dynamic_slice.20
  29.5 1.7 constant_dynamic-slice_fusion.8
  31.3 1.7 multiply_reduce_fusion.2
  33.0 0.3 select_add_fusion.2
  33.3 1.0 copy-done
  34.3 81.1 %all-reduce.3.cloned.1.call-done = f32[1024,256]{1,0:T(8,128)} async-done(((f32[1024,256]{1,0:T(8,128)}), f32[1024,256]{1,0:T(8,128)}) %all-reduce.3.cloned.1.call-update) | async-done | bytes 1048592 | tf_op jit(solution)/shard_map/psum | solution.py:42
  115.4 3.4 %fusion.54 = f32[256,256]{1,0:T(8,128)S(1)} fusion(f32[1024,256]{1,0:T(8,128)} %all-reduce.3.cloned.1.call-done), kind=kOutput, calls=%fused_computation.98 | convolution fusion | flops 805306368 | bytes 1310720 | tf_op jit(solution)/shard_map/dot_general | solution.py:43
  118.9 2.4 %all-gather = f32[512,256]{1,0:T(8,128)S(1)} all-gather(f32[256,256]{1,0:T(8,128)S(1)} %fusion.54), channel_id=2, replica_groups=mesh['grp'=2,'yz'=8,'gx'=2] {'gx'}, dimensions={0}, use_global_device_ids=true | all-gather | bytes 786432 | tf_op jit(solution)/shard_map/all_gather | solution.py:46
  121.5 11.7 %cholesky.50 = f32[128,128]{1,0:T(8,128)S(1)} custom-call(f32[128,128]{1,0:T(8,128)S(1)} %cholesky.118), custom_call_target="Cholesky" | custom-call | tf_op jit(solution)/shard_map/jit(cholesky)/cholesky | solution.py:48
  133.2 0.6 compare_reduce_fusion.1
  133.9 9.8 %custom-call.14 = f32[1,128,128]{1,2,0:T(8,128)S(1)} custom-call(f32[1,128,128]{2,1,0:T(8,128)S(1)} %get-tuple-element.132), custom_call_target="InvertDiagBlocksLowerTriangular" | custom-call | tf_op jit(solution)/shard_map/jit(cholesky)/cholesky | solution.py:48
  143.7 0.2 constant_dynamic-update-slice_fusion.1
  143.9 0.3 convolution_subtract_fusion.1
  144.2 11.7 %cholesky.105 = f32[128,128]{1,0:T(8,128)S(1)} custom-call(f32[128,128]{1,0:T(8,128)S(1)} %convolution_subtract_fusion.1), custom_call_target="Cholesky" | custom-call | tf_op jit(solution)/shard_map/jit(cholesky)/cholesky | solution.py:48
  155.9 0.7 compare_reduce_fusion
  158.1 4.3 %while.12 = (s32[]{:T(128)}, f32[256,256]{1,0:T(8,128)S(1)}, s32[2,2]{1,0:T(2,128)S(1)}, f32[2,128,128]{2,1,0:T(8,128)S(1)}, s32[]{:T(128)}) while((s32[]{:T(128)}, f32[256,256]{1,0:T(8,128)S(1)}, s32[2,2]{1,0:T(2,128)S(1)}, f32[2,128,128]{2,1,0:T(8,128)S(1)}, s32[]{:T(128)}) %tuple.59), condition=%wide.while_cond, body=%wide.while_body.sunk | while | flops 2 | bytes 131189 | solution.py:49
  158.3 0.6 fusion.64
  158.9 1.4 bitcast_dynamic-update-slice_fusion.2
  160.3 0.6 fusion.64
  160.9 1.4 bitcast_dynamic-update-slice_fusion.2
  162.4 19.7 %custom-call.15 = f32[2,128,128]{1,2,0:T(8,128)S(1)} custom-call(f32[2,128,128]{2,1,0:T(8,128)S(1)} %get-tuple-element.42), custom_call_target="InvertDiagBlocksLowerTriangular" | custom-call | tf_op jit(solution)/shard_map/triangular_solve | solution.py:49
  182.0 0.6 fusion.32
  182.7 1.0 convolution_subtract_fusion
  183.7 0.6 fusion.36
  184.3 8.3 %fusion.29 = f32[256,4096]{1,0:T(8,128)} fusion(bf16[128,8,32,128]{3,2,1,0:T(8,128)(2,1)} %bitcast.55, f32[1024,128]{0,1:T(8,128)S(1)} %fusion.36, f32[1024,128]{0,1:T(8,128)S(1)} %fusion.32), kind=kOutput, calls=%fused_computation.38 | convolution fusion | flops 2148532224 | bytes 13631488 | tf_op jit(solution)/shard_map/dot_general | solution.py:56
  192.7 1.3 copy.9
  194.0 10.4 %reduce-scatter.2.cloned.1.call-done = f32[128,4096]{1,0:T(8,128)} async-done(((f32[256,4096]{1,0:T(8,128)}), f32[128,4096]{1,0:T(8,128)}) %reduce-scatter.2.cloned.1.call-update) | async-done | bytes 2097168 | tf_op jit(solution)/shard_map/reduce_scatter | solution.py:55
  204.4 1.8 convert_bitcast_fusion
  206.2 1.2 copy.12
  (27 shorter events, 0.7 us)
Async XLA Ops:
  7.2 108.2 %all-reduce.3.cloned.1.call-start = ((), (), s32[]{:S(2)}) async-start(), calls=%async_computation.1 | async-start | bytes 2097152 | tf_op jit(solution)/shard_map/psum | solution.py:42
  33.3 1.0 copy-start
  34.3 170.1 %reduce-scatter.2.cloned.1.call-start = ((), (), s32[]{:S(2)}) async-start(), calls=%async_computation.2 | async-start | bytes 6291456 | tf_op jit(solution)/shard_map/reduce_scatter | solution.py:55
  115.4 66.6 %copy-start.1 = (f32[1024,256]{1,0:T(8,128)S(1)}, f32[1024,256]{1,0:T(8,128)}, u32[]{:S(2)}) copy-start(f32[1024,256]{1,0:T(8,128)} %all-reduce.3.cloned.1.call-done) | copy-start | bytes 3145732
Sparse Core Ops, SparseCore 0:
  34.4 80.9 all-reduce.2
  192.7 11.6 reduce-scatter.1
